TPU v7x, 512 devices: a whole 4x4x16 slice. The times are simulated.
512 devices in a mesh: leaf: 128 (over z, x, core), vec: 4 (over y).
Axes of the slice: x: 4, y: 4, z: 16, core: 2. Of those that a mesh axis runs over, the one named last changes fastest.
Arguments:
- samples: bfloat16 [64, 524288], P('vec', 'leaf'), may hold values from -6 to 6
- coords: float32 [3, 524288], P(None, 'leaf'), may hold values from -4 to 4
- panel_area: float32 [524288], P('leaf'), may hold values from 0.05 to 0.5
- quad_weight: float32 [524288], P('leaf'), may hold values from 0.2 to 1
- leaf_basis: bfloat16 [2048, 64, 256], P('leaf'), may hold values from -0.375 to 0.375
- transfer: bfloat16 [1024, 2, 64, 64], P('leaf'), may hold values from -0.5 to 0.5
- coupling_fine: bfloat16 [2048, 16, 64, 64], P('leaf'), may hold values from -0.1875 to 0.1875
- coupling_coarse: bfloat16 [1024, 16, 64, 64], P('leaf'), may hold values from -0.1875 to 0.1875
- near_list: int32 [2048, 16], P('leaf'), may hold values from 0 to 2047, as said below
- send_fine: int32 [16384, 2], P('leaf'), may hold values from 0 to 15
- send_coarse: int32 [16384, 1], P('leaf'), may hold values from 0 to 7
- far_fine: int32 [2048, 16], P('leaf'), may hold values from 0 to 255, as said below
- far_coarse: int32 [1024, 16], P('leaf'), may hold values from 0 to 127, as said below
Outputs:
- sample_out: bfloat16 [64, 524288], P('vec', 'leaf')
- sample_gram: float32 [2048, 64, 64], P('leaf', 'vec')
Inputs may be any that keep to these rules, and one draw needn't show every extreme that they name: `near_list`: row g names 16 different leaves, each at most 16 leaves from g. `send_fine`: row e * 128 + d names clusters of device e, counted on e from 0; every slot carries one. `send_coarse`: row e * 128 + d names clusters of device e, counted on e from 0; every slot carries one. `far_fine`: the rows of one device's 16 leaves name each of the values 0 to 255 exactly once. `far_coarse`: the rows of one device's parents name each of the values 0 to 127 exactly once.
All inputs are finite; a program needn't handle non-finite values.
Results may differ from a plain program's by a relative error of at most 0.0085.
Values may be sent and summed in bfloat16 or wider, within the bound.
No kernel may reach another device: no remote copies, remote signals or barrier semaphores. Data moves between devices by JAX's collectives and lax.ppermute only.
A program may use at most 64 MiB of HBM per device.

v0:
```python
import jax
import jax.numpy as jnp
from jax import lax
from jax.sharding import PartitionSpec as P

LEAF = 256
HW = 16
four_pi = 4.0 * 3.141592653589793


def extended(block, sides, width):
    for axis, dim in sides:
        count = lax.axis_size(axis)
        forward = [(i, i + 1) for i in range(count - 1)]
        backward = [(target, source) for source, target in forward]
        low = lax.ppermute(
            lax.slice_in_dim(block, block.shape[dim] - width, None, axis=dim), axis, forward
        )
        high = lax.ppermute(lax.slice_in_dim(block, 0, width, axis=dim), axis, backward)
        block = jnp.concatenate([low, block, high], axis=dim)
    return block


def laid_out(blocks, dim):
    dims = list(blocks.shape[1:])
    dims[dim] *= blocks.shape[0]
    return jnp.moveaxis(blocks, 0, dim).reshape(dims)


def copy_for_each(array, axis):
    copies = jnp.broadcast_to(array, (lax.axis_size(axis), *array.shape))
    return lax.all_to_all(copies, axis, split_axis=0, concat_axis=0, tiled=True)


def gathered_copies(array, axis, dim):
    return laid_out(copy_for_each(array, axis), dim)


def kernel_block(target, source):
    delta_x = target[0][:, None] - source[0][None, :]
    delta_y = target[1][:, None] - source[1][None, :]
    delta_z = target[2][:, None] - source[2][None, :]
    distance = delta_x * delta_x + delta_y * delta_y + delta_z * delta_z + source[3][None, :]
    return (source[4][None, :] / (four_pi * jnp.sqrt(distance))).astype(jnp.bfloat16)


def apply_coupling(tile_set, received, far_list, vec_dev, basis_rank):
    coef_table = received.reshape(-1, vec_dev, basis_rank)
    picked = coef_table[far_list]
    return jnp.einsum("ibkl,ibvl->ivk", tile_set, picked, preferred_element_type=jnp.float32)


def near_leaves(leaf_ids, window, geo_leaves, vec_leaves, targets):

    def one_leaf(index):
        chosen = window[index]
        src_geo = jnp.take(geo_leaves, chosen, axis=1)
        src_vec = jnp.take(vec_leaves, chosen, axis=1)
        target = lax.dynamic_index_in_dim(targets, index, 1, keepdims=False)
        blocks = jax.vmap(kernel_block, (None, 1))(target, src_geo)
        return jnp.einsum("npq,vnq->vp", blocks, src_vec, preferred_element_type=jnp.float32)

    return lax.map(one_leaf, leaf_ids)


def per_device(
    samples,
    coords,
    panel_area,
    quad_weight,
    leaf_basis,
    transfer,
    coupling_fine,
    coupling_coarse,
    near_list,
    send_fine,
    send_coarse,
    far_fine,
    far_coarse,
):
    vec_dev, points = samples.shape
    leaf_dev, basis_rank, leaf_pts = leaf_basis.shape
    devices = lax.axis_size("leaf")
    device = lax.axis_index("leaf")
    geometry = jnp.concatenate([coords, panel_area[None, :], quad_weight[None, :]], axis=0)
    geo_wide = extended(geometry, (("leaf", 1),), HW * leaf_pts)
    vec_wide = extended(samples, (("leaf", 1),), HW * leaf_pts)
    geo_leaves = geo_wide.reshape(5, -1, leaf_pts)
    window = near_list - (device * leaf_dev - HW)
    targets = coords.reshape(3, leaf_dev, leaf_pts)
    local_rows = samples.reshape(vec_dev, leaf_dev, leaf_pts)
    fine_coef = jnp.einsum(
        "ikp,vip->ivk", leaf_basis, local_rows, preferred_element_type=jnp.float32
    ).astype(jnp.bfloat16)
    coarse_coef = jnp.einsum(
        "mskl,msvk->mvl",
        transfer,
        fine_coef.reshape(-1, 2, vec_dev, basis_rank),
        preferred_element_type=jnp.float32,
    ).astype(jnp.bfloat16)
    send_leafs = fine_coef[send_fine].reshape(devices, -1, vec_dev * basis_rank)
    send_parents = coarse_coef[send_coarse].reshape(devices, -1, vec_dev * basis_rank)
    got_leafs = lax.all_to_all(send_leafs, "leaf", split_axis=0, concat_axis=0, tiled=True)
    got_parents = lax.all_to_all(send_parents, "leaf", split_axis=0, concat_axis=0, tiled=True)
    vec_groups = lax.axis_size("vec")
    quarter = leaf_dev // vec_groups
    all_wide = gathered_copies(vec_wide, "vec", 0)
    all_leaves = all_wide.reshape(all_wide.shape[0], -1, leaf_pts)
    first_leaf = lax.axis_index("vec") * quarter
    leaf_ids = first_leaf + jnp.arange(quarter, dtype=jnp.int32)
    near_quarter = near_leaves(leaf_ids, window, geo_leaves, all_leaves, targets)
    near_part = lax.all_to_all(
        near_quarter.astype(jnp.bfloat16), "vec", split_axis=1, concat_axis=0, tiled=True
    ).astype(near_quarter.dtype)
    field_fine = apply_coupling(coupling_fine, got_leafs, far_fine, vec_dev, basis_rank)
    field_coarse = apply_coupling(
        coupling_coarse, got_parents, far_coarse, vec_dev, basis_rank
    ).astype(jnp.bfloat16)
    pushed = jnp.einsum(
        "mskl,mvl->msvk", transfer, field_coarse, preferred_element_type=jnp.float32
    )
    local_field = (field_fine + pushed.reshape(leaf_dev, vec_dev, basis_rank)).astype(jnp.bfloat16)
    far_part = jnp.einsum(
        "ikp,ivk->vip", leaf_basis, local_field, preferred_element_type=jnp.float32
    )
    sample_out = (
        (jnp.transpose(near_part, (1, 0, 2)) + far_part)
        .reshape(vec_dev, points)
        .astype(jnp.bfloat16)
    )
    own_rows = sample_out.reshape(vec_dev, leaf_dev, leaf_pts)
    shard_rows = gathered_copies(sample_out, "vec", 0)
    shaped = shard_rows.reshape(shard_rows.shape[0], leaf_dev, leaf_pts)
    sample_gram = jnp.einsum(
        "vip,wip->ivw", own_rows, shaped, preferred_element_type=jnp.float32
    ) * (1.0 / LEAF)
    return (sample_out, sample_gram)


def solution(mesh):
    return jax.shard_map(
        per_device,
        mesh=mesh,
        in_specs=(
            P("vec", "leaf"),
            P(None, "leaf"),
            P("leaf"),
            P("leaf"),
            P("leaf", None, None),
            P("leaf", None, None, None),
            P("leaf", None, None, None),
            P("leaf", None, None, None),
            P("leaf", None),
            P("leaf", None),
            P("leaf", None),
            P("leaf", None),
            P("leaf", None),
        ),
        out_specs=(P("vec", "leaf"), P("leaf", "vec", None)),
        check_vma=False,
    )
```

profile of v0, /device:TPU:32, one launch (start us, length us, event | category | flops | bytes accessed | tf_op | source)
XLA Modules:
  0.0 212.3 jit_solution(4894522826093835305)
XLA Ops:
  0.7 3.8 %collective-permute-start.1 = (bf16[16,4096]{1,0:T(8,128)(2,1)}, bf16[16,4096]{1,0:T(8,128)(2,1)}, u32[]{:S(2)}, u32[]{:S(2)}) collective-permute-start(bf16[16,4096]{1,0:T(8,128)(2,1)} %param.15), channel_id=1, source_target_pairs={{4,0},{8,4},{12,8},{16,12},{20,16},{24,20},{28,24},{32,28},{36,32}... | collective-permute-start | bytes 393224 | tf_op jit(solution)/shard_map/ppermute | solution.py:19
  4.5 1.9 collective-permute-start
  6.4 0.9 pad_maximum_fusion.2
  7.3 5.8 %collective-permute-start.3 = (f32[5,4096]{1,0:T(8,128)S(1)}, f32[5,4096]{1,0:T(8,128)S(1)}, u32[]{:S(2)}, u32[]{:S(2)}) collective-permute-start(f32[5,4096]{1,0:T(8,128)S(1)} %pad_maximum_fusion.2), channel_id=1, source_target_pairs={{4,0},{8,4},{12,8},{16,12},{20,16},{24,20},{28,24},{32,28},{36,32}... | collective-permute-start | bytes 245768 | tf_op jit(solution)/shard_map/ppermute | solution.py:19
  13.1 1.9 collective-permute-start.2
  16.3 1.3 broadcast_subtract_fusion
  17.6 1.3 convolution_convert_fusion
  19.0 1.2 fusion.12
  20.2 1.5 copy.72
  21.7 0.7 gather_fusion.4
  23.4 0.7 reduce
  24.3 0.9 reshape.159
  26.5 1.0 pad_maximum_fusion
  27.5 1.2 broadcast_in_dim.52
  28.8 4.5 %all-to-all-start = ((bf16[4,16,12288]{2,1,0:T(8,128)(2,1)}), bf16[4,16,12288]{2,1,0:T(8,128)(2,1)}, u32[]{:S(2)}, u32[]{:S(2)}) async-start(bf16[4,16,12288]{2,1,0:T(8,128)(2,1)} %broadcast_in_dim.52), calls=%async_computation | async-start | bytes 3145728 | tf_op jit(solution)/shard_map/all_to_all | solution.py:32
  33.3 1.0 pad_maximum_fusion.1
  34.3 17.8 %all-to-all-done = bf16[4,16,12288]{2,1,0:T(8,128)(2,1)} async-done(((bf16[4,16,12288]{2,1,0:T(8,128)(2,1)}), bf16[4,16,12288]{2,1,0:T(8,128)(2,1)}, u32[]{:S(2)}, u32[]{:S(2)}) %all-to-all-start) | async-done | bytes 1572896 | tf_op jit(solution)/shard_map/all_to_all | solution.py:32
  52.1 19.6 %all-to-all-start.3 = ((bf16[128,2,512]{2,1,0:T(2,128)(2,1)}), bf16[128,2,512]{2,1,0:T(2,128)(2,1)S(1)}, u32[]{:S(2)}, u32[]{:S(2)}) async-start(bf16[128,2,512]{2,1,0:T(2,128)(2,1)} %reshape.159), calls=%async_computation.3 | async-start | bytes 524288 | tf_op jit(solution)/shard_map/all_to_all | solution.py:104
  71.7 1.7 copy.56
  73.5 1.7 copy.32
  75.2 54.8 %while.10 = (s32[]{:T(128)}, bf16[4,64,256]{2,0,1:T(4,128)(2,1)}, s32[4]{0:T(128)}, s32[16,16]{1,0:T(8,128)}, bf16[64,48,256]{2,0,1:T(8,128)(2,1)}, /*index=5*/f...) while((s32[]{:T(128)}, bf16[4,64,256]{2,0,1:T(4,128)(2,1)}, ...), condition=%wide.region_1.2_spmd, body=%wide.region_0.1_spmd.sunk | while | flops 147084432 | bytes 3536671 | solution.py:63
  75.2 1.2 dynamic_slice.21
  78.2 0.7 fusion.36
  79.4 0.7 compare_and_fusion.2
  80.3 1.3 constant_dynamic-slice_fusion.5
  81.7 2.0 gather_fusion.1
  83.7 3.6 %fusion.38 = bf16[1,64,256]{2,1,0:T(8,128)(2,1)S(1)} fusion(f32[16,256]{1,0:T(8,128)S(1)} %get-tuple-element.137, f32[16,256]{1,0:T(8,128)S(1)} %get-tuple-element.138, f32[256]{0:T(256)} %bitcast.153, f32[16,256]{1,0:T(8,128)S(1)} %get-tuple-element.142, f32[256]{0:T(256)} %bitcast.152, f32[16,256]{1,0:T(8,128)S(1)} %get-tuple-element.144, ...), kind=kOutput, calls=%fused_computation.8.clone.1 | convolution fusion | flops 147062784 | bytes 642064 | tf_op jit(solution)/shard_map/while/body/eval_jaxpr/npq,vnq->vp/dot_general | solution.py:61
  87.4 0.9 dynamic_update_slice.5
  88.9 1.2 dynamic_slice.21
  91.9 0.7 fusion.36
  93.1 0.7 compare_and_fusion.2
  94.0 1.3 constant_dynamic-slice_fusion.5
  95.4 2.0 gather_fusion.1
  97.4 3.6 %fusion.38 = bf16[1,64,256]{2,1,0:T(8,128)(2,1)S(1)} fusion(f32[16,256]{1,0:T(8,128)S(1)} %get-tuple-element.137, f32[16,256]{1,0:T(8,128)S(1)} %get-tuple-element.138, f32[256]{0:T(256)} %bitcast.153, f32[16,256]{1,0:T(8,128)S(1)} %get-tuple-element.142, f32[256]{0:T(256)} %bitcast.152, f32[16,256]{1,0:T(8,128)S(1)} %get-tuple-element.144, ...), kind=kOutput, calls=%fused_computation.8.clone.1 | convolution fusion | flops 147062784 | bytes 642064 | tf_op jit(solution)/shard_map/while/body/eval_jaxpr/npq,vnq->vp/dot_general | solution.py:61
  101.1 0.9 dynamic_update_slice.5
  102.6 1.2 dynamic_slice.21
  106.8 0.7 compare_and_fusion.2
  107.7 1.3 constant_dynamic-slice_fusion.5
  109.1 2.0 gather_fusion.1
  111.1 3.6 %fusion.38 = bf16[1,64,256]{2,1,0:T(8,128)(2,1)S(1)} fusion(f32[16,256]{1,0:T(8,128)S(1)} %get-tuple-element.137, f32[16,256]{1,0:T(8,128)S(1)} %get-tuple-element.138, f32[256]{0:T(256)} %bitcast.153, f32[16,256]{1,0:T(8,128)S(1)} %get-tuple-element.142, f32[256]{0:T(256)} %bitcast.152, f32[16,256]{1,0:T(8,128)S(1)} %get-tuple-element.144, ...), kind=kOutput, calls=%fused_computation.8.clone.1 | convolution fusion | flops 147062784 | bytes 642064 | tf_op jit(solution)/shard_map/while/body/eval_jaxpr/npq,vnq->vp/dot_general | solution.py:61
  114.8 0.9 dynamic_update_slice.5
  116.3 1.2 dynamic_slice.21
  119.3 0.7 fusion.36
  120.6 0.7 compare_and_fusion.2
  121.4 1.3 constant_dynamic-slice_fusion.5
  122.8 2.0 gather_fusion.1
  124.8 3.6 %fusion.38 = bf16[1,64,256]{2,1,0:T(8,128)(2,1)S(1)} fusion(f32[16,256]{1,0:T(8,128)S(1)} %get-tuple-element.137, f32[16,256]{1,0:T(8,128)S(1)} %get-tuple-element.138, f32[256]{0:T(256)} %bitcast.153, f32[16,256]{1,0:T(8,128)S(1)} %get-tuple-element.142, f32[256]{0:T(256)} %bitcast.152, f32[16,256]{1,0:T(8,128)S(1)} %get-tuple-element.144, ...), kind=kOutput, calls=%fused_computation.8.clone.1 | convolution fusion | flops 147062784 | bytes 642064 | tf_op jit(solution)/shard_map/while/body/eval_jaxpr/npq,vnq->vp/dot_general | solution.py:61
  128.5 0.9 dynamic_update_slice.5
  130.0 0.7 copy-done.2
  130.7 4.1 %all-to-all-start.1 = ((bf16[4,64,256]{2,0,1:T(4,128)(2,1)}), bf16[4,64,256]{2,0,1:T(4,128)(2,1)}, u32[]{:S(2)}, u32[]{:S(2)}) async-start(bf16[4,64,256]{2,0,1:T(4,128)(2,1)} %get-tuple-element.39), calls=%async_computation.1 | async-start | bytes 262144 | tf_op jit(solution)/shard_map/all_to_all | solution.py:112
  135.5 0.8 gather_fusion.2
  136.3 1.4 reshape.89
  137.7 3.2 %all-to-all-done.1 = bf16[4,64,256]{2,0,1:T(4,128)(2,1)} async-done(((bf16[4,64,256]{2,0,1:T(4,128)(2,1)}), bf16[4,64,256]{2,0,1:T(4,128)(2,1)}, u32[]{:S(2)}, u32[]{:S(2)}) %all-to-all-start.1) | async-done | bytes 131104 | tf_op jit(solution)/shard_map/all_to_all | solution.py:112
  140.9 16.6 %all-to-all-start.2 = ((bf16[128,2,1024]{2,1,0:T(2,128)(2,1)}), bf16[128,2,1024]{2,1,0:T(2,128)(2,1)}, u32[]{:S(2)}, u32[]{:S(2)}) async-start(bf16[128,2,1024]{2,1,0:T(2,128)(2,1)} %reshape.89), calls=%async_computation.2 | async-start | bytes 1048576 | tf_op jit(solution)/shard_map/all_to_all | solution.py:103
  157.7 2.2 %reshape.160 = bf16[128,1,1024]{2,1,0:T(2,128)(2,1)S(1)} reshape(bf16[128,2,512]{2,1,0:T(2,128)(2,1)} %copy-done.2) | data formatting | bytes 524288
  160.7 0.7 gather_fusion.5
  161.4 1.5 fusion.15
  163.0 0.9 copy.34
  163.9 26.2 %all-to-all-done.2 = bf16[128,2,1024]{2,1,0:T(2,128)(2,1)} async-done(((bf16[128,2,1024]{2,1,0:T(2,128)(2,1)}), bf16[128,2,1024]{2,1,0:T(2,128)(2,1)}, u32[]{:S(2)}, u32[]{:S(2)}) %all-to-all-start.2) | async-done | bytes 524320 | tf_op jit(solution)/shard_map/all_to_all | solution.py:103
  190.1 2.3 %reshape.90 = bf16[256,16,64]{2,1,0:T(8,128)(2,1)S(1)} reshape(bf16[128,2,1024]{2,1,0:T(2,128)(2,1)} %all-to-all-done.2) | data formatting | bytes 1048576 | tf_op jit(solution)/shard_map/reshape | solution.py:48
  192.4 1.8 gather_fusion.3
  194.2 4.0 %fusion.9 = bf16[16,16,256]{2,1,0:T(8,128)(2,1)S(1)} fusion(f32[16,16,256]{2,1,0:T(8,128)S(1)} %bitcast.140, bf16[16,64,256]{2,1,0:T(8,128)(2,1)} %param.19, f32[16,16,64]{2,1,0:T(8,128)} %bitcast.142, bf16[16,16,16,64]{3,2,1,0:T(8,128)(2,1)} %bitcast.132, bf16[16,16,64,64]{3,2,1,0:T(8,128)(2,1)} %param.21), kind=kOutput, calls=%fused_computation.31 | convolution fusion | flops 42106880 | bytes 3604480 | tf_op jit(solution)/shard_map/ikp,ivk->vip/dot_general | solution.py:123
  198.2 13.0 %all_to_all.29 = bf16[4,16,4096]{2,1,0:T(8,128)(2,1)S(1)} all-to-all(bf16[4,16,4096]{2,1,0:T(8,128)(2,1)S(1)} %broadcast_in_dim.59), channel_id=1, replica_groups=mesh['leaf'=128,'vec'=4] {'vec'}, dimensions={0} | all-to-all | bytes 1048576 | tf_op jit(solution)/shard_map/all_to_all | solution.py:32
  211.4 0.9 convolution_multiply_fusion
  (101 shorter events, 12.2 us)
Async XLA Ops:
  0.6 160.8 %copy-start = (bf16[8,16,64,64]{3,2,1,0:T(8,128)(2,1)S(1)}, bf16[8,16,64,64]{3,2,1,0:T(8,128)(2,1)}, u32[]{:S(2)}) copy-start(bf16[8,16,64,64]{3,2,1,0:T(8,128)(2,1)} %param.22) | copy-start | bytes 3145732
  0.6 25.9 %copy-start.5 = (bf16[16,4096]{1,0:T(8,128)(2,1)S(1)}, bf16[16,4096]{1,0:T(8,128)(2,1)}, u32[]{:S(2)}) copy-start(bf16[16,4096]{1,0:T(8,128)(2,1)} %param.15) | copy-start | bytes 393220
  0.7 25.9 %collective-permute-start.1 = (bf16[16,4096]{1,0:T(8,128)(2,1)}, bf16[16,4096]{1,0:T(8,128)(2,1)}, u32[]{:S(2)}, u32[]{:S(2)}) collective-permute-start(bf16[16,4096]{1,0:T(8,128)(2,1)} %param.15), channel_id=1, source_target_pairs={{4,0},{8,4},{12,8},{16,12},{20,16},{24,20},{28,24},{32,28},{36,32}... | collective-permute-start | bytes 393224 | tf_op jit(solution)/shard_map/ppermute | solution.py:19
  4.5 22.1 %collective-permute-start = (bf16[16,4096]{1,0:T(8,128)(2,1)}, bf16[16,4096]{1,0:T(8,128)(2,1)}, u32[]{:S(2)}, u32[]{:S(2)}) collective-permute-start(bf16[16,4096]{1,0:T(8,128)(2,1)} %param.15), channel_id=1, source_target_pairs={{0,4},{4,8},{8,12},{12,16},{16,20},{20,24},{24,28},{28,32},{32,36}... | collective-permute-start | bytes 393224 | tf_op jit(solution)/shard_map/ppermute | solution.py:16
  7.3 25.9 %collective-permute-start.3 = (f32[5,4096]{1,0:T(8,128)S(1)}, f32[5,4096]{1,0:T(8,128)S(1)}, u32[]{:S(2)}, u32[]{:S(2)}) collective-permute-start(f32[5,4096]{1,0:T(8,128)S(1)} %pad_maximum_fusion.2), channel_id=1, source_target_pairs={{4,0},{8,4},{12,8},{16,12},{20,16},{24,20},{28,24},{32,28},{36,32}... | collective-permute-start | bytes 245768 | tf_op jit(solution)/shard_map/ppermute | solution.py:19
  13.1 20.2 %collective-permute-start.2 = (f32[5,4096]{1,0:T(8,128)S(1)}, f32[5,4096]{1,0:T(8,128)}, u32[]{:S(2)}, u32[]{:S(2)}) collective-permute-start(f32[5,4096]{1,0:T(8,128)S(1)} %pad_maximum_fusion.2), channel_id=1, source_target_pairs={{0,4},{4,8},{8,12},{12,16},{16,20},{20,24},{24,28},{28,32},{32,36}... | collective-permute-start | bytes 245768 | tf_op jit(solution)/shard_map/ppermute | solution.py:16
  22.4 10.9 %copy-start.3 = (f32[3,4096]{1,0:T(4,128)S(1)}, f32[3,4096]{1,0:T(4,128)}, u32[]{:S(2)}) copy-start(f32[3,4096]{1,0:T(4,128)} %param.16) | copy-start | bytes 147460
  22.4 10.9 %copy-start.8 = (f32[4096]{0:T(1024)S(1)}, f32[4096]{0:T(1024)}, u32[]{:S(2)}) copy-start(f32[4096]{0:T(1024)} %param.18) | copy-start | bytes 49156
  28.8 23.3 %all-to-all-start = ((bf16[4,16,12288]{2,1,0:T(8,128)(2,1)}), bf16[4,16,12288]{2,1,0:T(8,128)(2,1)}, u32[]{:S(2)}, u32[]{:S(2)}) async-start(bf16[4,16,12288]{2,1,0:T(8,128)(2,1)} %broadcast_in_dim.52), calls=%async_computation | async-start | bytes 3145728 | tf_op jit(solution)/shard_map/all_to_all | solution.py:32
  52.1 77.9 %all-to-all-start.3 = ((bf16[128,2,512]{2,1,0:T(2,128)(2,1)}), bf16[128,2,512]{2,1,0:T(2,128)(2,1)S(1)}, u32[]{:S(2)}, u32[]{:S(2)}) async-start(bf16[128,2,512]{2,1,0:T(2,128)(2,1)} %reshape.159), calls=%async_computation.3 | async-start | bytes 524288 | tf_op jit(solution)/shard_map/all_to_all | solution.py:104
  80.1 1.5 copy-start.9
  83.7 3.7 %copy-start.6 = (bf16[4,64,256]{2,0,1:T(4,128)(2,1)S(1)}, bf16[4,64,256]{2,0,1:T(4,128)(2,1)}, u32[]{:S(2)}) copy-start(bf16[4,64,256]{2,0,1:T(4,128)(2,1)} %get-tuple-element.160) | copy-start | bytes 393220 | tf_op jit(solution)/shard_map/while
  88.3 0.7 copy-start.7
  93.8 1.5 copy-start.9
  97.4 3.7 %copy-start.6 = (bf16[4,64,256]{2,0,1:T(4,128)(2,1)S(1)}, bf16[4,64,256]{2,0,1:T(4,128)(2,1)}, u32[]{:S(2)}) copy-start(bf16[4,64,256]{2,0,1:T(4,128)(2,1)} %get-tuple-element.160) | copy-start | bytes 393220 | tf_op jit(solution)/shard_map/while
  102.0 0.7 copy-start.7
  107.5 1.5 copy-start.9
  111.1 3.7 %copy-start.6 = (bf16[4,64,256]{2,0,1:T(4,128)(2,1)S(1)}, bf16[4,64,256]{2,0,1:T(4,128)(2,1)}, u32[]{:S(2)}) copy-start(bf16[4,64,256]{2,0,1:T(4,128)(2,1)} %get-tuple-element.160) | copy-start | bytes 393220 | tf_op jit(solution)/shard_map/while
  115.7 0.7 copy-start.7
  121.2 1.5 copy-start.9
  124.8 3.7 %copy-start.6 = (bf16[4,64,256]{2,0,1:T(4,128)(2,1)S(1)}, bf16[4,64,256]{2,0,1:T(4,128)(2,1)}, u32[]{:S(2)}) copy-start(bf16[4,64,256]{2,0,1:T(4,128)(2,1)} %get-tuple-element.160) | copy-start | bytes 393220 | tf_op jit(solution)/shard_map/while
  129.4 0.7 copy-start.7
  130.0 27.4 %copy-start.11 = (s32[8,16]{1,0:T(8,128)S(1)}, s32[8,16]{1,0:T(8,128)}, u32[]{:S(2)}) copy-start(s32[8,16]{1,0:T(8,128)} %param.27) | copy-start | bytes 1540
  130.0 27.5 %copy-start.10 = (s32[16,16]{1,0:T(8,128)S(1)}, s32[16,16]{1,0:T(8,128)}, u32[]{:S(2)}) copy-start(s32[16,16]{1,0:T(8,128)} %param.26) | copy-start | bytes 3076
  130.0 0.7 copy-start.2
  130.7 30.7 %copy-start.1 = (bf16[8,2,64,64]{3,2,1,0:T(8,128)(2,1)S(1)}, bf16[8,2,64,64]{3,2,1,0:T(8,128)(2,1)}, u32[]{:S(2)}) copy-start(bf16[8,2,64,64]{3,2,1,0:T(8,128)(2,1)} %param.20) | copy-start | bytes 393220
  130.7 10.1 %all-to-all-start.1 = ((bf16[4,64,256]{2,0,1:T(4,128)(2,1)}), bf16[4,64,256]{2,0,1:T(4,128)(2,1)}, u32[]{:S(2)}, u32[]{:S(2)}) async-start(bf16[4,64,256]{2,0,1:T(4,128)(2,1)} %get-tuple-element.39), calls=%async_computation.1 | async-start | bytes 262144 | tf_op jit(solution)/shard_map/all_to_all | solution.py:112
  140.9 49.3 %all-to-all-start.2 = ((bf16[128,2,1024]{2,1,0:T(2,128)(2,1)}), bf16[128,2,1024]{2,1,0:T(2,128)(2,1)}, u32[]{:S(2)}, u32[]{:S(2)}) async-start(bf16[128,2,1024]{2,1,0:T(2,128)(2,1)} %reshape.89), calls=%async_computation.2 | async-start | bytes 1048576 | tf_op jit(solution)/shard_map/all_to_all | solution.py:103
  198.2 14.1 %copy-start.4 = (bf16[16,2,8,256]{3,2,0,1:T(8,128)(2,1)}, bf16[16,2,8,256]{3,2,0,1:T(8,128)(2,1)S(1)}, u32[]{:S(2)}) copy-start(bf16[16,2,8,256]{3,2,0,1:T(8,128)(2,1)S(1)} %copy.55) | copy-start | bytes 393220
where the time goes:
time: 214 us; the launch traced here: 212 us
  starting transfers between devices  58.1 us (27%)
  local copies, waits for them, and re-layouts  48.9 us (23%)
  waiting for transfers between devices  47.2 us (22%)
  matrix products  23.4 us (11%)
  other arithmetic  13.4 us (6%)
  blocking collectives  13 us (6%)
  loops' own time  7.29 us (3%)
    all_to_all x1, waiting for transfers between devices, per_device(): lax.all_to_all(send_leafs, 'leaf', split_axis=0, concat_axis=0, tiled=True)  26.2 us
    all_to_all x1, starting transfers between devices, per_device(): lax.all_to_all(send_parents, 'leaf', split_axis=0, concat_axis=0, tiled=T...  19.6 us
    all_to_all x1, waiting for transfers between devices, copy_for_each(): return lax.all_to_all(copies, axis, split_axis=0, concat_axis=0, tiled=True)  17.8 us
    all_to_all x1, starting transfers between devices, per_device(): lax.all_to_all(send_leafs, 'leaf', split_axis=0, concat_axis=0, tiled=True)  16.6 us
    dot_general x4, matrix products, one_leaf(): jnp.einsum('npq,vnq->vp', blocks, src_vec, preferred_element_type=jnp.flo...  14.5 us
    all_to_all x1, blocking collectives, copy_for_each(): return lax.all_to_all(copies, axis, split_axis=0, concat_axis=0, tiled=True)  13 us
    ppermute x2, starting transfers between devices, extended(): lax.ppermute(lax.slice_in_dim(block, 0, width, axis=dim), axis, backward)  9.54 us
    gather x4, local copies, waits for them, and re-layouts, one_leaf(): src_vec = jnp.take(vec_leaves, chosen, axis=1)  7.95 us
  transfers between devices with their start and end apart: 8, of which 3 were waited for; matrix products, arithmetic and copies ran while one was open for 34% of the time, Pallas kernels for 0%

commit v1 on v0

--- a/solution.py
+++ b/solution.py
@@ -109,8 +109,14 @@
     first_leaf = lax.axis_index("vec") * quarter
     leaf_ids = first_leaf + jnp.arange(quarter, dtype=jnp.int32)
     near_quarter = near_leaves(leaf_ids, window, geo_leaves, all_leaves, targets)
-    near_part = lax.all_to_all(
-        near_quarter.astype(jnp.bfloat16), "vec", split_axis=1, concat_axis=0, tiled=True
+    near_part = jnp.concatenate(
+        lax.all_to_all(
+            jnp.stack(jnp.split(near_quarter.astype(jnp.bfloat16), lax.axis_size("vec"), axis=1)),
+            "vec",
+            0,
+            0,
+        ),
+        axis=0,
     ).astype(near_quarter.dtype)
     field_fine = apply_coupling(coupling_fine, got_leafs, far_fine, vec_dev, basis_rank)
     field_coarse = apply_coupling(

time: 214 us -> 190 us (0.89)
  the two profiles are of different devices: /device:TPU:32 before, /device:TPU:2 now
where the time goes in v1:
time: 190 us; the launch traced here: 188 us
  starting transfers between devices  49.5 us (26%)
  local copies, waits for them, and re-layouts  44.1 us (23%)
  waiting for transfers between devices  30.9 us (16%)
  matrix products  26.5 us (14%)
  blocking collectives  14.1 us (7%)
  other arithmetic  13.6 us (7%)
  loops' own time  7.96 us (4%)
    all_to_all x1, starting transfers between devices, per_device(): lax.all_to_all(send_parents, 'leaf', split_axis=0, concat_axis=0, tiled=T...  21 us
    dot_general x4, matrix products, one_leaf(): jnp.einsum('npq,vnq->vp', blocks, src_vec, preferred_element_type=jnp.flo...  17.1 us
    all_to_all x1, waiting for transfers between devices, copy_for_each(): return lax.all_to_all(copies, axis, split_axis=0, concat_axis=0, tiled=True)  15.9 us
    all_to_all x1, waiting for transfers between devices, per_device(): lax.all_to_all(send_parents, 'leaf', split_axis=0, concat_axis=0, tiled=T...  15 us
    all_to_all x1, blocking collectives, copy_for_each(): return lax.all_to_all(copies, axis, split_axis=0, concat_axis=0, tiled=True)  14.1 us
    ppermute x2, starting transfers between devices, extended(): lax.ppermute(lax.slice_in_dim(block, 0, width, axis=dim), axis, backward)  9.87 us
    gather x4, local copies, waits for them, and re-layouts, one_leaf(): src_vec = jnp.take(vec_leaves, chosen, axis=1)  8.44 us
    another operation x1, loops' own time, near_leaves(): return lax.map(one_leaf, leaf_ids)  7.96 us
  transfers between devices with their start and end apart: 8, of which 2 were waited for; matrix products, arithmetic and copies ran while one was open for 41% of the time, Pallas kernels for 0%

profile of v1, /device:TPU:2, one launch (start us, length us, event | category | flops | bytes accessed | tf_op | source)
XLA Modules:
  0.0 187.7 jit_solution(15907688334695866129)
XLA Ops:
  0.7 1.7 pad_maximum_fusion.2
  2.4 1.9 %collective-permute-start.2 = (f32[5,4096]{1,0:T(8,128)}, f32[5,4096]{1,0:T(8,128)}, u32[]{:S(2)}, u32[]{:S(2)}) collective-permute-start(f32[5,4096]{1,0:T(8,128)} %pad_maximum_fusion.2), channel_id=1, source_target_pairs={{0,4},{4,8},{8,12},{12,16},{16,20},{20,24},{24,28},{28,32},{32,36}... | collective-permute-start | bytes 245768 | tf_op jit(solution)/shard_map/ppermute | solution.py:16
  4.3 3.6 %collective-permute-start.3 = (f32[5,4096]{1,0:T(8,128)}, f32[5,4096]{1,0:T(8,128)}, u32[]{:S(2)}, u32[]{:S(2)}) collective-permute-start(f32[5,4096]{1,0:T(8,128)} %pad_maximum_fusion.2), channel_id=1, source_target_pairs={{4,0},{8,4},{12,8},{16,12},{20,16},{24,20},{28,24},{32,28},{36,32}... | collective-permute-start | bytes 245768 | tf_op jit(solution)/shard_map/ppermute | solution.py:19
  8.0 1.9 %collective-permute-start = (bf16[16,4096]{1,0:T(8,128)(2,1)}, bf16[16,4096]{1,0:T(8,128)(2,1)}, u32[]{:S(2)}, u32[]{:S(2)}) collective-permute-start(bf16[16,4096]{1,0:T(8,128)(2,1)} %param.15), channel_id=1, source_target_pairs={{0,4},{4,8},{8,12},{12,16},{16,20},{20,24},{24,28},{28,32},{32,36}... | collective-permute-start | bytes 393224 | tf_op jit(solution)/shard_map/ppermute | solution.py:16
  9.9 6.2 %collective-permute-start.1 = (bf16[16,4096]{1,0:T(8,128)(2,1)}, bf16[16,4096]{1,0:T(8,128)(2,1)}, u32[]{:S(2)}, u32[]{:S(2)}) collective-permute-start(bf16[16,4096]{1,0:T(8,128)(2,1)} %param.15), channel_id=1, source_target_pairs={{4,0},{8,4},{12,8},{16,12},{20,16},{24,20},{28,24},{32,28},{36,32}... | collective-permute-start | bytes 393224 | tf_op jit(solution)/shard_map/ppermute | solution.py:19
  16.1 0.7 fusion.21
  16.8 1.3 convolution_convert_fusion
  18.2 1.2 fusion.13
  19.4 0.7 gather_fusion.4
  21.1 0.8 reduce
  22.0 0.9 reshape.157
  22.9 21.0 %all-to-all-start.3 = ((bf16[128,2,512]{2,1,0:T(2,128)(2,1)}), bf16[128,2,512]{2,1,0:T(2,128)(2,1)S(1)}, u32[]{:S(2)}, u32[]{:S(2)}) async-start(bf16[128,2,512]{2,1,0:T(2,128)(2,1)} %reshape.157), calls=%async_computation.3 | async-start | bytes 524288 | tf_op jit(solution)/shard_map/all_to_all | solution.py:104
  46.1 0.6 copy.65
  46.7 0.8 gather_fusion.2
  47.6 1.4 reshape.88
  49.1 1.1 pad_maximum_fusion
  50.2 15.0 %all-to-all-done.3 = bf16[128,2,512]{2,1,0:T(2,128)(2,1)S(1)} async-done(((bf16[128,2,512]{2,1,0:T(2,128)(2,1)}), bf16[128,2,512]{2,1,0:T(2,128)(2,1)S(1)}, u32[]{:S(2)}, u32[]{:S(2)}) %all-to-all-start.3) | async-done | bytes 262176 | tf_op jit(solution)/shard_map/all_to_all | solution.py:104
  65.2 1.2 broadcast_in_dim.52
  66.4 4.5 %all-to-all-start = ((bf16[4,16,12288]{2,1,0:T(8,128)(2,1)}), bf16[4,16,12288]{2,1,0:T(8,128)(2,1)}, u32[]{:S(2)}, u32[]{:S(2)}) async-start(bf16[4,16,12288]{2,1,0:T(8,128)(2,1)} %broadcast_in_dim.52), calls=%async_computation | async-start | bytes 3145728 | tf_op jit(solution)/shard_map/all_to_all | solution.py:32
  70.9 1.0 pad_maximum_fusion.1
  72.0 2.2 %reshape.158 = bf16[128,1,1024]{2,1,0:T(2,128)(2,1)S(1)} reshape(bf16[128,2,512]{2,1,0:T(2,128)(2,1)} %copy-done.2) | data formatting | bytes 524288
  75.0 1.5 gather_fusion.5
  76.5 15.9 %all-to-all-done = bf16[4,16,12288]{2,1,0:T(8,128)(2,1)} async-done(((bf16[4,16,12288]{2,1,0:T(8,128)(2,1)}), bf16[4,16,12288]{2,1,0:T(8,128)(2,1)}, u32[]{:S(2)}, u32[]{:S(2)}) %all-to-all-start) | async-done | bytes 1572896 | tf_op jit(solution)/shard_map/all_to_all | solution.py:32
  92.4 7.0 %all-to-all-start.2 = ((bf16[128,2,1024]{2,1,0:T(2,128)(2,1)}), bf16[128,2,1024]{2,1,0:T(2,128)(2,1)S(1)}, u32[]{:S(2)}, u32[]{:S(2)}) async-start(bf16[128,2,1024]{2,1,0:T(2,128)(2,1)} %reshape.88), calls=%async_computation.2 | async-start | bytes 1048576 | tf_op jit(solution)/shard_map/all_to_all | solution.py:103
  99.4 1.7 copy.49
  101.2 1.8 copy.29
  102.9 54.8 %while.10 = (s32[]{:T(128)}, bf16[4,64,256]{2,1,0:T(8,128)(2,1)}, s32[4]{0:T(128)}, s32[16,16]{1,0:T(8,128)}, bf16[64,48,256]{2,0,1:T(8,128)(2,1)}, /*index=5*/f...) while((s32[]{:T(128)}, bf16[4,64,256]{2,1,0:T(8,128)(2,1)}, ...), condition=%wide.region_1.2_spmd, body=%wide.region_0.1_spmd.sunk | while | flops 147084432 | bytes 2407143 | solution.py:63
  102.9 1.2 dynamic_slice.21
  106.1 0.7 fusion.37
  107.4 0.7 compare_and_fusion.2
  108.8 0.6 copy_bitcast_fusion.8
  109.5 2.1 %gather_fusion.1 = bf16[16,64,256]{2,1,0:T(8,128)(2,1)S(1)} fusion(bf16[64,48,256]{2,0,1:T(8,128)(2,1)} %get-tuple-element.179, s32[1024]{0:T(1024)} %copy-done.6), kind=kCustom, calls=%fused_computation.clone.1 | custom fusion | bytes 1048640 | tf_op jit(solution)/shard_map/while/body/eval_jaxpr/jit(_take)/gather | solution.py:58
  111.6 0.7 constant_dynamic-slice_fusion.5
  112.3 4.3 %fusion.39 = bf16[4,64,256]{2,1,0:T(8,128)(2,1)} fusion(bf16[4,64,256]{2,1,0:T(8,128)(2,1)} %get-tuple-element.164, s32[]{:T(128)} %get-tuple-element.163, f32[16,256]{1,0:T(8,128)} %get-tuple-element.141, f32[16,256]{1,0:T(8,128)} %get-tuple-element.142, f32[256]{0:T(256)S(1)} %bitcast.161, f32[16,256]{1,0:T(8,128)} %get-tuple-element.146, ...), kind=kOutput, calls=%fused_computation.9.clone.1 | convolution fusion | flops 147062784 | bytes 675840 | tf_op jit(solution)/shard_map/while/body/eval_jaxpr/npq,vnq->vp/dot_general | solution.py:61
  116.6 1.2 dynamic_slice.21
  119.8 0.7 fusion.37
  121.1 0.7 compare_and_fusion.2
  122.5 0.6 copy_bitcast_fusion.8
  123.2 2.1 %gather_fusion.1 = bf16[16,64,256]{2,1,0:T(8,128)(2,1)S(1)} fusion(bf16[64,48,256]{2,0,1:T(8,128)(2,1)} %get-tuple-element.179, s32[1024]{0:T(1024)} %copy-done.6), kind=kCustom, calls=%fused_computation.clone.1 | custom fusion | bytes 1048640 | tf_op jit(solution)/shard_map/while/body/eval_jaxpr/jit(_take)/gather | solution.py:58
  125.3 0.7 constant_dynamic-slice_fusion.5
  126.0 4.3 %fusion.39 = bf16[4,64,256]{2,1,0:T(8,128)(2,1)} fusion(bf16[4,64,256]{2,1,0:T(8,128)(2,1)} %get-tuple-element.164, s32[]{:T(128)} %get-tuple-element.163, f32[16,256]{1,0:T(8,128)} %get-tuple-element.141, f32[16,256]{1,0:T(8,128)} %get-tuple-element.142, f32[256]{0:T(256)S(1)} %bitcast.161, f32[16,256]{1,0:T(8,128)} %get-tuple-element.146, ...), kind=kOutput, calls=%fused_computation.9.clone.1 | convolution fusion | flops 147062784 | bytes 675840 | tf_op jit(solution)/shard_map/while/body/eval_jaxpr/npq,vnq->vp/dot_general | solution.py:61
  130.3 1.2 dynamic_slice.21
  133.5 0.7 fusion.37
  134.8 0.7 compare_and_fusion.2
  136.2 0.6 copy_bitcast_fusion.8
  136.8 2.1 %gather_fusion.1 = bf16[16,64,256]{2,1,0:T(8,128)(2,1)S(1)} fusion(bf16[64,48,256]{2,0,1:T(8,128)(2,1)} %get-tuple-element.179, s32[1024]{0:T(1024)} %copy-done.6), kind=kCustom, calls=%fused_computation.clone.1 | custom fusion | bytes 1048640 | tf_op jit(solution)/shard_map/while/body/eval_jaxpr/jit(_take)/gather | solution.py:58
  139.0 0.7 constant_dynamic-slice_fusion.5
  139.7 4.3 %fusion.39 = bf16[4,64,256]{2,1,0:T(8,128)(2,1)} fusion(bf16[4,64,256]{2,1,0:T(8,128)(2,1)} %get-tuple-element.164, s32[]{:T(128)} %get-tuple-element.163, f32[16,256]{1,0:T(8,128)} %get-tuple-element.141, f32[16,256]{1,0:T(8,128)} %get-tuple-element.142, f32[256]{0:T(256)S(1)} %bitcast.161, f32[16,256]{1,0:T(8,128)} %get-tuple-element.146, ...), kind=kOutput, calls=%fused_computation.9.clone.1 | convolution fusion | flops 147062784 | bytes 675840 | tf_op jit(solution)/shard_map/while/body/eval_jaxpr/npq,vnq->vp/dot_general | solution.py:61
  144.0 1.2 dynamic_slice.21
  147.2 0.7 fusion.37
  148.5 0.7 compare_and_fusion.2
  149.9 0.6 copy_bitcast_fusion.8
  150.5 2.1 %gather_fusion.1 = bf16[16,64,256]{2,1,0:T(8,128)(2,1)S(1)} fusion(bf16[64,48,256]{2,0,1:T(8,128)(2,1)} %get-tuple-element.179, s32[1024]{0:T(1024)} %copy-done.6), kind=kCustom, calls=%fused_computation.clone.1 | custom fusion | bytes 1048640 | tf_op jit(solution)/shard_map/while/body/eval_jaxpr/jit(_take)/gather | solution.py:58
  152.7 0.7 constant_dynamic-slice_fusion.5
  153.4 4.3 %fusion.39 = bf16[4,64,256]{2,1,0:T(8,128)(2,1)} fusion(bf16[4,64,256]{2,1,0:T(8,128)(2,1)} %get-tuple-element.164, s32[]{:T(128)} %get-tuple-element.163, f32[16,256]{1,0:T(8,128)} %get-tuple-element.141, f32[16,256]{1,0:T(8,128)} %get-tuple-element.142, f32[256]{0:T(256)S(1)} %bitcast.161, f32[16,256]{1,0:T(8,128)} %get-tuple-element.146, ...), kind=kOutput, calls=%fused_computation.9.clone.1 | convolution fusion | flops 147062784 | bytes 675840 | tf_op jit(solution)/shard_map/while/body/eval_jaxpr/npq,vnq->vp/dot_general | solution.py:61
  157.7 0.8 slice_bitcast_fusion.3
  158.5 0.7 pad_maximum_fusion.3
  159.2 3.3 %all-to-all-start.1 = ((bf16[4,4,16,256]{3,2,1,0:T(8,128)(2,1)}), bf16[4,4,16,256]{3,2,1,0:T(8,128)(2,1)S(1)}, u32[]{:S(2)}, u32[]{:S(2)}) async-start(bf16[4,4,16,256]{3,2,1,0:T(8,128)(2,1)} %pad_maximum_fusion.3), calls=%async_computation.1 | async-start | bytes 262144 | tf_op jit(solution)/shard_map/all_to_all | solution.py:113
  162.6 1.9 %fusion.16 = f32[8,16,2,64]{3,1,2,0:T(8,128)S(1)} fusion(bf16[8,2,64,64]{3,2,1,0:T(8,128)(2,1)} %param.20, bf16[8,16,16,64]{3,2,1,0:T(8,128)(2,1)} %bitcast.142, bf16[8,16,64,64]{3,2,1,0:T(8,128)(2,1)S(1)} %copy-done), kind=kOutput, calls=%fused_computation.43 | convolution fusion | flops 18882560 | bytes 1507328 | tf_op jit(solution)/shard_map/mskl,mvl->msvk/dot_general | solution.py:125
  164.5 2.3 %reshape.89 = bf16[256,16,64]{2,1,0:T(8,128)(2,1)S(1)} reshape(bf16[128,2,1024]{2,1,0:T(2,128)(2,1)} %copy-done.1) | data formatting | bytes 1048576 | tf_op jit(solution)/shard_map/reshape | solution.py:48
  166.8 1.8 gather_fusion.3
  168.6 3.9 %fusion.10 = bf16[16,16,256]{2,1,0:T(8,128)(2,1)S(1)} fusion(bf16[16,64,256]{2,1,0:T(8,128)(2,1)} %param.19, f32[16,16,64]{2,1,0:T(8,128)S(1)} %bitcast.148, bf16[16,16,16,64]{3,2,1,0:T(8,128)(2,1)} %bitcast.139, bf16[16,16,64,64]{3,2,1,0:T(8,128)(2,1)} %param.21, bf16[16,16,256]{2,1,0:T(8,128)(2,1)S(1)} %bitcast.151), kind=kOutput, calls=%fused_computation.32 | convolution fusion | flops 42172416 | bytes 3473408 | tf_op jit(solution)/shard_map/ikp,ivk->vip/dot_general | solution.py:129
  172.6 14.1 %all_to_all.25 = bf16[4,16,4096]{2,1,0:T(8,128)(2,1)S(1)} all-to-all(bf16[4,16,4096]{2,1,0:T(8,128)(2,1)S(1)} %broadcast_in_dim.59), channel_id=1, replica_groups=mesh['leaf'=128,'vec'=4] {'vec'}, dimensions={0} | all-to-all | bytes 1048576 | tf_op jit(solution)/shard_map/all_to_all | solution.py:32
  186.7 0.9 convolution_multiply_fusion
  (94 shorter events, 9.8 us)
Async XLA Ops:
  0.6 161.9 %copy-start = (bf16[8,16,64,64]{3,2,1,0:T(8,128)(2,1)S(1)}, bf16[8,16,64,64]{3,2,1,0:T(8,128)(2,1)}, u32[]{:S(2)}) copy-start(bf16[8,16,64,64]{3,2,1,0:T(8,128)(2,1)} %param.22) | copy-start | bytes 3145732
  0.6 45.5 %copy-start.3 = (f32[3,4096]{1,0:T(4,128)S(1)}, f32[3,4096]{1,0:T(4,128)}, u32[]{:S(2)}) copy-start(f32[3,4096]{1,0:T(4,128)} %param.16) | copy-start | bytes 147460
  0.7 43.3 %copy-start.14 = (s32[128,2]{0,1:T(2,128)S(1)}, s32[128,2]{0,1:T(2,128)}, u32[]{:S(2)}) copy-start(s32[128,2]{0,1:T(2,128)} %param.24) | copy-start | bytes 3076
  0.7 43.6 %copy-start.11 = (s32[16,16]{1,0:T(8,128)S(1)}, s32[16,16]{1,0:T(8,128)}, u32[]{:S(2)}) copy-start(s32[16,16]{1,0:T(8,128)} %param.26) | copy-start | bytes 3076
  0.7 44.3 %copy-start.13 = (s32[8,16]{1,0:T(8,128)S(1)}, s32[8,16]{1,0:T(8,128)}, u32[]{:S(2)}) copy-start(s32[8,16]{1,0:T(8,128)} %param.27) | copy-start | bytes 1540
  0.7 44.3 %copy-start.12 = (s32[16,16]{1,0:T(8,128)S(1)}, s32[16,16]{1,0:T(8,128)}, u32[]{:S(2)}) copy-start(s32[16,16]{1,0:T(8,128)} %param.23) | copy-start | bytes 3076
  2.4 68.5 %collective-permute-start.2 = (f32[5,4096]{1,0:T(8,128)}, f32[5,4096]{1,0:T(8,128)}, u32[]{:S(2)}, u32[]{:S(2)}) collective-permute-start(f32[5,4096]{1,0:T(8,128)} %pad_maximum_fusion.2), channel_id=1, source_target_pairs={{0,4},{4,8},{8,12},{12,16},{16,20},{20,24},{24,28},{28,32},{32,36}... | collective-permute-start | bytes 245768 | tf_op jit(solution)/shard_map/ppermute | solution.py:16
  4.3 66.6 %collective-permute-start.3 = (f32[5,4096]{1,0:T(8,128)}, f32[5,4096]{1,0:T(8,128)}, u32[]{:S(2)}, u32[]{:S(2)}) collective-permute-start(f32[5,4096]{1,0:T(8,128)} %pad_maximum_fusion.2), channel_id=1, source_target_pairs={{4,0},{8,4},{12,8},{16,12},{20,16},{24,20},{28,24},{32,28},{36,32}... | collective-permute-start | bytes 245768 | tf_op jit(solution)/shard_map/ppermute | solution.py:19
  8.0 41.1 %collective-permute-start = (bf16[16,4096]{1,0:T(8,128)(2,1)}, bf16[16,4096]{1,0:T(8,128)(2,1)}, u32[]{:S(2)}, u32[]{:S(2)}) collective-permute-start(bf16[16,4096]{1,0:T(8,128)(2,1)} %param.15), channel_id=1, source_target_pairs={{0,4},{4,8},{8,12},{12,16},{16,20},{20,24},{24,28},{28,32},{32,36}... | collective-permute-start | bytes 393224 | tf_op jit(solution)/shard_map/ppermute | solution.py:16
  9.9 39.2 %collective-permute-start.1 = (bf16[16,4096]{1,0:T(8,128)(2,1)}, bf16[16,4096]{1,0:T(8,128)(2,1)}, u32[]{:S(2)}, u32[]{:S(2)}) collective-permute-start(bf16[16,4096]{1,0:T(8,128)(2,1)} %param.15), channel_id=1, source_target_pairs={{4,0},{8,4},{12,8},{16,12},{20,16},{24,20},{28,24},{32,28},{36,32}... | collective-permute-start | bytes 393224 | tf_op jit(solution)/shard_map/ppermute | solution.py:19
  22.9 42.3 %all-to-all-start.3 = ((bf16[128,2,512]{2,1,0:T(2,128)(2,1)}), bf16[128,2,512]{2,1,0:T(2,128)(2,1)S(1)}, u32[]{:S(2)}, u32[]{:S(2)}) async-start(bf16[128,2,512]{2,1,0:T(2,128)(2,1)} %reshape.157), calls=%async_computation.3 | async-start | bytes 524288 | tf_op jit(solution)/shard_map/all_to_all | solution.py:104
  47.6 23.3 %copy-start.7 = (f32[4096]{0:T(1024)S(1)}, f32[4096]{0:T(1024)}, u32[]{:S(2)}) copy-start(f32[4096]{0:T(1024)} %param.18) | copy-start | bytes 49156
  49.0 21.9 %copy-start.4 = (f32[3,4096]{1,0:T(4,128)S(1)}, f32[3,4096]{1,0:T(4,128)}, u32[]{:S(2)}) copy-start(f32[3,4096]{1,0:T(4,128)} %param.16) | copy-start | bytes 147460
  49.0 21.9 %copy-start.8 = (f32[4096]{0:T(1024)S(1)}, f32[4096]{0:T(1024)}, u32[]{:S(2)}) copy-start(f32[4096]{0:T(1024)} %param.17) | copy-start | bytes 49156
  65.2 5.7 %copy-start.2 = (bf16[128,2,512]{2,1,0:T(2,128)(2,1)}, bf16[128,2,512]{2,1,0:T(2,128)(2,1)S(1)}, u32[]{:S(2)}) copy-start(bf16[128,2,512]{2,1,0:T(2,128)(2,1)S(1)} %all-to-all-done.3) | copy-start | bytes 786436
  66.4 26.0 %all-to-all-start = ((bf16[4,16,12288]{2,1,0:T(8,128)(2,1)}), bf16[4,16,12288]{2,1,0:T(8,128)(2,1)}, u32[]{:S(2)}, u32[]{:S(2)}) async-start(bf16[4,16,12288]{2,1,0:T(8,128)(2,1)} %broadcast_in_dim.52), calls=%async_computation | async-start | bytes 3145728 | tf_op jit(solution)/shard_map/all_to_all | solution.py:32
  92.4 66.8 %all-to-all-start.2 = ((bf16[128,2,1024]{2,1,0:T(2,128)(2,1)}), bf16[128,2,1024]{2,1,0:T(2,128)(2,1)S(1)}, u32[]{:S(2)}, u32[]{:S(2)}) async-start(bf16[128,2,1024]{2,1,0:T(2,128)(2,1)} %reshape.88), calls=%async_computation.2 | async-start | bytes 1048576 | tf_op jit(solution)/shard_map/all_to_all | solution.py:103
  106.8 2.7 %copy-start.6 = (s32[1024]{0:T(1024)}, s32[1024]{0:T(1024)S(1)}, u32[]{:S(2)}) copy-start(s32[1024]{0:T(1024)S(1)} %pad_clamp_fusion.6) | copy-start | bytes 12292 | tf_op jit(solution)/shard_map/while
  108.1 1.4 copy-start.10
  120.5 2.7 %copy-start.6 = (s32[1024]{0:T(1024)}, s32[1024]{0:T(1024)S(1)}, u32[]{:S(2)}) copy-start(s32[1024]{0:T(1024)S(1)} %pad_clamp_fusion.6) | copy-start | bytes 12292 | tf_op jit(solution)/shard_map/while
  121.8 1.4 copy-start.10
  134.2 2.7 %copy-start.6 = (s32[1024]{0:T(1024)}, s32[1024]{0:T(1024)S(1)}, u32[]{:S(2)}) copy-start(s32[1024]{0:T(1024)S(1)} %pad_clamp_fusion.6) | copy-start | bytes 12292 | tf_op jit(solution)/shard_map/while
  135.5 1.4 copy-start.10
  147.9 2.7 %copy-start.6 = (s32[1024]{0:T(1024)}, s32[1024]{0:T(1024)S(1)}, u32[]{:S(2)}) copy-start(s32[1024]{0:T(1024)S(1)} %pad_clamp_fusion.6) | copy-start | bytes 12292 | tf_op jit(solution)/shard_map/while
  149.1 1.4 copy-start.10
  157.7 9.1 %copy-start.9 = (s32[1024]{0:T(1024)S(1)}, s32[1024]{0:T(1024)}, u32[]{:S(2)}) copy-start(s32[1024]{0:T(1024)} %pad_clamp_fusion.3) | copy-start | bytes 12292
  159.2 3.3 %copy-start.1 = (bf16[128,2,1024]{2,1,0:T(2,128)(2,1)}, bf16[128,2,1024]{2,1,0:T(2,128)(2,1)S(1)}, u32[]{:S(2)}) copy-start(bf16[128,2,1024]{2,1,0:T(2,128)(2,1)S(1)} %all-to-all-done.2) | copy-start | bytes 1572868
  159.2 9.4 %all-to-all-start.1 = ((bf16[4,4,16,256]{3,2,1,0:T(8,128)(2,1)}), bf16[4,4,16,256]{3,2,1,0:T(8,128)(2,1)S(1)}, u32[]{:S(2)}, u32[]{:S(2)}) async-start(bf16[4,4,16,256]{3,2,1,0:T(8,128)(2,1)} %pad_maximum_fusion.3), calls=%async_computation.1 | async-start | bytes 262144 | tf_op jit(solution)/shard_map/all_to_all | solution.py:113
  172.5 15.1 %copy-start.5 = (bf16[16,2,8,256]{3,2,0,1:T(8,128)(2,1)}, bf16[16,2,8,256]{3,2,0,1:T(8,128)(2,1)S(1)}, u32[]{:S(2)}) copy-start(bf16[16,2,8,256]{3,2,0,1:T(8,128)(2,1)S(1)} %copy.48) | copy-start | bytes 393220
